TPU v7x, 256 devices: a whole 4x4x8 slice. The times are simulated.
256 devices in a mesh: copy: 4 (over x_hi, core), space: 64 (over y, z, x_lo).
Axes of the slice: x: 4 (x_hi: 2, x_lo: 2; x = x_hi * 2 + x_lo), y: 4, z: 8, core: 2. Of those that a mesh axis runs over, the one named last changes fastest.
Arguments:
- noisy_tokens: bfloat16 [4, 256, 256, 384], P('copy', 'space'), may hold values from -6 to 6
- grad_out: bfloat16 [4, 256, 256, 384], P('copy', 'space'), may hold values from -6 to 6
- filter_weight: bfloat16 [2, 256, 256, 384], P(None, None, 'space'), may hold values from -4 to 4
- weight_in: bfloat16 [384, 1536], replicated, may hold values from -0.3125 to 0.3125
- weight_out: bfloat16 [1536, 384], replicated, may hold values from -0.15625 to 0.15625
- gain_one: float32 [384], replicated, may hold values from 0.1 to 1.9
- gain_two: float32 [384], replicated, may hold values from 0.1 to 1.9
Outputs:
- block_out: bfloat16 [4, 256, 256, 384], P('copy', 'space')
- grad_tokens: bfloat16 [4, 256, 256, 384], P('copy', 'space')
- grad_filter: float32 [2, 256, 256, 384], P(None, None, 'space')
- grad_weight_in: bfloat16 [384, 1536], replicated
- grad_weight_out: bfloat16 [1536, 384], replicated
- grad_gain_one: float32 [384], replicated
- grad_gain_two: float32 [384], replicated
All inputs are finite; a program needn't handle non-finite values.
Results may differ from a plain program's by a relative error of at most 0.024.
Values may be sent and summed in bfloat16 or wider, within the bound.
A program may use at most 128 MiB of HBM per device.

v0:
```python
import math
import jax
import jax.numpy as jnp
from jax import lax
from jax.sharding import PartitionSpec as P

EPS = 1e-06


def dft_parts(length):
    index = jnp.arange(length, dtype=jnp.int32)
    phase = index[:, None] * index[None, :] % length
    angle = phase.astype(jnp.float32) * (2.0 * math.pi / length)
    factor = 1.0 / math.sqrt(length)
    return (
        (jnp.cos(angle) * factor).astype(jnp.bfloat16),
        (jnp.sin(angle) * factor).astype(jnp.bfloat16),
    )


def row_table(length):
    cosine, sine = dft_parts(length)
    return jnp.stack([cosine, -sine])


def column_table(length, direction):
    cosine, sine = dft_parts(length)
    upper = jnp.stack([cosine, direction * sine], axis=1)
    lower = jnp.stack([-direction * sine, cosine], axis=1)
    return jnp.stack([upper, lower])


def layer_norm(values):
    centre = jnp.mean(values, axis=-1, keepdims=True)
    centred = values - centre
    variance = jnp.mean(centred * centred, axis=-1, keepdims=True)
    rstd_value = lax.rsqrt(variance + EPS)
    return (centred * rstd_value, rstd_value)


def norm_backward(upstream, normed, rstd_value, gain):
    scaled = upstream * gain
    result = (
        scaled
        - jnp.mean(scaled, axis=-1, keepdims=True)
        - normed * jnp.mean(scaled * normed, axis=-1, keepdims=True)
    ) * rstd_value
    lead = tuple(range(upstream.ndim - 1))
    return (result, jnp.sum(upstream * normed, axis=lead))


def apply_filter(spectrum, filter_weight, direction):
    real_part = spectrum[0].astype(jnp.float32)
    imag_part = spectrum[1].astype(jnp.float32)
    kernel_real = filter_weight[0].astype(jnp.float32)
    kernel_imag = direction * filter_weight[1].astype(jnp.float32)
    return jnp.stack(
        [
            kernel_real * real_part - kernel_imag * imag_part,
            kernel_real * imag_part + kernel_imag * real_part,
        ]
    )


def exact_gelu(values):
    return jax.nn.gelu(values, approximate=False)


def spectral(values, filter_weight, direction):
    width = values.shape[2]
    rows_tab = row_table(width)
    rows = jnp.einsum(
        "pkw,bhwc->pbhkc", rows_tab, values, preferred_element_type=jnp.float32
    ).astype(jnp.bfloat16)
    columns = lax.all_to_all(rows, "space", split_axis=3, concat_axis=2, tiled=True)
    height = columns.shape[2]
    spectrum = jnp.einsum(
        "qmph,pbhkc->qbmkc", column_table(height, 1), columns, preferred_element_type=jnp.float32
    ).astype(jnp.bfloat16)
    weighted = apply_filter(spectrum, filter_weight[:, None], direction).astype(jnp.bfloat16)
    returned = jnp.einsum(
        "qmph,pbhkc->qbmkc", column_table(height, -1), weighted, preferred_element_type=jnp.float32
    ).astype(jnp.bfloat16)
    back_rows = lax.all_to_all(returned, "space", split_axis=2, concat_axis=3, tiled=True)
    output = jnp.einsum("pkw,pbhkc->bhwc", rows_tab, back_rows, preferred_element_type=jnp.float32)
    return (output, spectrum)


def body(noisy_tokens, grad_out, filter_weight, weight_in, weight_out, gain_one, gain_two):
    batch, rows_dev, width, chans = noisy_tokens.shape
    inputs = noisy_tokens.astype(jnp.float32)
    normed_one, rstd_one = layer_norm(inputs)
    mixed_in = (normed_one * gain_one).astype(jnp.bfloat16)
    spatial, spectrum = spectral(mixed_in, filter_weight, 1)
    normed_two, rstd_two = layer_norm(spatial)
    mlp_in = (normed_two * gain_two).astype(jnp.bfloat16).reshape(-1, chans)
    preact = jnp.dot(mlp_in, weight_in, preferred_element_type=jnp.float32)
    activated = exact_gelu(preact).astype(jnp.bfloat16)
    mlp_out = jnp.dot(activated, weight_out, preferred_element_type=jnp.float32)
    block_out = (inputs + mlp_out.reshape(inputs.shape)).astype(jnp.bfloat16)
    upstream = grad_out.reshape(-1, chans)
    grad_act = jnp.dot(upstream, weight_out.T, preferred_element_type=jnp.float32)
    grad_pre = jax.vjp(exact_gelu, preact)[1](grad_act)[0].astype(jnp.bfloat16)
    sum_out = jnp.dot(activated.T, upstream, preferred_element_type=jnp.float32)
    sum_in = jnp.dot(mlp_in.T, grad_pre, preferred_element_type=jnp.float32)
    grad_mlp = jnp.dot(grad_pre, weight_in.T, preferred_element_type=jnp.float32).reshape(
        inputs.shape
    )
    grad_spatial, sum_gain_two = norm_backward(grad_mlp, normed_two, rstd_two, gain_two)
    back_spatial, adjoint = spectral(grad_spatial.astype(jnp.bfloat16), filter_weight, -1)
    spec_f = spectrum.astype(jnp.float32)
    adj_f = adjoint.astype(jnp.float32)
    filter_terms = jnp.stack(
        [
            jnp.sum(adj_f[0] * spec_f[0] + adj_f[1] * spec_f[1], axis=0),
            jnp.sum(adj_f[1] * spec_f[0] - adj_f[0] * spec_f[1], axis=0),
        ]
    )
    grad_filter = lax.psum(filter_terms.astype(jnp.bfloat16), "copy").astype(jnp.float32)
    grad_normed, sum_gain_one = norm_backward(back_spatial, normed_one, rstd_one, gain_one)
    grad_tokens = (grad_out.astype(jnp.float32) + grad_normed).astype(jnp.bfloat16)
    local_sums = (sum_in, sum_out, sum_gain_one, sum_gain_two)
    summed = lax.psum(
        (local_sums[0], local_sums[1], local_sums[2], local_sums[3]), ("copy", "space")
    )
    total_tokens = batch * lax.axis_size("copy") * rows_dev * lax.axis_size("space") * width
    factor = 1.0 / math.sqrt(total_tokens)
    return (
        block_out,
        grad_tokens,
        grad_filter,
        (summed[0] * factor).astype(jnp.bfloat16),
        (summed[1] * factor).astype(jnp.bfloat16),
        summed[2] * factor,
        summed[3] * factor,
    )


def solution(mesh):
    return jax.shard_map(
        body,
        mesh=mesh,
        in_specs=(
            P("copy", "space", None, None),
            P("copy", "space", None, None),
            P(None, None, "space", None),
            P(),
            P(),
            P(),
            P(),
        ),
        out_specs=(
            P("copy", "space", None, None),
            P("copy", "space", None, None),
            P(None, None, "space", None),
            P(),
            P(),
            P(),
            P(),
        ),
        check_vma=False,
    )
```

profile of v0, /device:TPU:1, one launch (start us, length us, event | category | flops | bytes accessed | tf_op | source)
XLA Modules:
  0.0 629.1 jit_solution(3767009619410764740)
XLA Ops:
  7.2 1.6 fusion.87
  8.8 1.6 multiply_convert_fusion.8
  10.5 1.4 copy.67
  12.8 0.6 fusion.39
  13.5 3.0 copy.69
  16.5 13.8 %all-to-all-start = ((bf16[2,1,4,256,384]{4,0,2,1,3:T(2,128)(2,1)}), bf16[2,1,4,256,384]{4,0,2,1,3:T(2,128)(2,1)}, u32[]{:S(2)}, u32[]{:S(2)}) async-start(bf16[2,1,4,256,384]{4,0,2,1,3:T(2,128)(2,1)} %copy.69), calls=%async_computation | async-start | bytes 3145728 | tf_op jit(solution)/shard_map/all_to_all | solution.py:75
  30.3 2.8 fusion.94
  33.1 0.6 copy.124
  33.8 1.8 copy.126
  35.6 1.0 broadcast_multiply_fusion
  36.6 1.1 multiply_convert_fusion.5
  37.7 1.0 fusion.74
  38.8 29.9 %all-to-all-done = bf16[2,1,4,256,384]{4,0,2,1,3:T(2,128)(2,1)} async-done(((bf16[2,1,4,256,384]{4,0,2,1,3:T(2,128)(2,1)}), bf16[2,1,4,256,384]{4,0,2,1,3:T(2,128)(2,1)}, u32[]{:S(2)}, u32[]{:S(2)}) %all-to-all-start) | async-done | bytes 1572896 | tf_op jit(solution)/shard_map/all_to_all | solution.py:75
  68.6 2.0 copy.70
  70.7 0.6 copy.71
  71.7 2.7 fusion.95
  74.4 0.6 fusion.26
  75.4 2.2 fusion.44
  77.6 4.3 copy.77
  81.9 45.2 %all_to_all.60 = bf16[2,1,256,4,384]{4,0,3,1,2:T(2,128)(2,1)S(1)} all-to-all(bf16[2,1,256,4,384]{4,0,3,1,2:T(2,128)(2,1)S(1)} %copy.77), channel_id=1, replica_groups=mesh['copy'=4,'space'=64] {'space'}, dimensions={2} | all-to-all | bytes 3145728 | tf_op jit(solution)/shard_map/all_to_all | solution.py:84
  127.2 0.6 copy.78
  128.3 1.4 reshape.561
  129.7 2.3 bitcast_reduce_fusion
  133.1 15.5 %multiply_convert_fusion = (bf16[1024,1536]{1,0:T(8,128)(2,1)}, f32[1024,1536]{1,0:T(8,128)S(1)}, f32[1024,1536]{1,0:T(8,128)S(1)}) fusion(bf16[1024,384]{1,0:T(8,128)(2,1)S(1)} %bitcast.255, bf16[384,1536]{1,0:T(8,128)(2,1)S(1)} %copy-done), kind=kOutput, calls=%fused_computation.3 | convolution fusion | flops 1310195712 | bytes 17694720 | tf_op jit(solution)/shard_map/dot_general | solution.py:97
  148.6 3.3 add_convert_fusion
  151.9 1.9 multiply_reduce_fusion.2
  153.8 1.1 multiply_reduce_fusion
  156.1 1.3 div.31
  157.4 4.0 fusion.40
  161.3 4.9 copy.84
  166.2 7.7 %all-to-all-start.2 = ((bf16[2,1,4,256,384]{4,0,2,1,3:T(2,128)(2,1)}), bf16[2,1,4,256,384]{4,0,2,1,3:T(2,128)(2,1)S(1)}, u32[]{:S(2)}, u32[]{:S(2)}) async-start(bf16[2,1,4,256,384]{4,0,2,1,3:T(2,128)(2,1)} %copy.84), calls=%async_computation.2 | async-start | bytes 3145728 | tf_op jit(solution)/shard_map/all_to_all | solution.py:75
  174.2 5.2 fusion.98
  179.3 3.2 fusion.99
  182.6 31.1 %all-to-all-done.2 = bf16[2,1,4,256,384]{4,0,2,1,3:T(2,128)(2,1)S(1)} async-done(((bf16[2,1,4,256,384]{4,0,2,1,3:T(2,128)(2,1)}), bf16[2,1,4,256,384]{4,0,2,1,3:T(2,128)(2,1)S(1)}, u32[]{:S(2)}, u32[]{:S(2)}) %all-to-all-start.2) | async-done | bytes 1572896 | tf_op jit(solution)/shard_map/all_to_all | solution.py:75
  213.7 0.6 copy.85
  214.3 0.6 copy.86
  214.9 2.6 copy.87
  217.5 4.3 fusion.96
  221.8 0.7 fusion.21
  222.9 1.0 fusion.50
  223.9 3.1 copy.90
  227.0 8.3 %all-to-all-start.3 = ((bf16[2,1,256,4,384]{4,0,3,1,2:T(2,128)(2,1)}), bf16[2,1,256,4,384]{4,0,3,1,2:T(2,128)(2,1)S(1)}, u32[]{:S(2)}, u32[]{:S(2)}) async-start(bf16[2,1,256,4,384]{4,0,3,1,2:T(2,128)(2,1)} %copy.90), calls=%async_computation.3 | async-start | bytes 3145728 | tf_op jit(solution)/shard_map/all_to_all | solution.py:84
  235.6 3.4 fusion.57
  239.5 1.0 copy-done.2
  240.4 0.6 fusion.58
  241.0 1.3 pad_maximum_fusion
  242.4 2.3 copy.82
  244.7 5.1 fusion.97
  249.8 3.1 copy.81
  252.9 215.0 %all-reduce.7.cloned.1.call-done = (f32[384,1536]{1,0:T(8,128)}, f32[1536,384]{1,0:T(8,128)}) async-done(((f32[384,1536]{1,0:T(8,128)}, f32[1536,384]{1,0:T(8,128)}), (f32[384,1536]{1,0:T(8,128)}, f32[1536,384]{1,0:T(8,128)})) %all-reduce.7.cloned.1.call-update) | async-done | bytes 4718608 | tf_op jit(solution)/shard_map/psum | solution.py:123
  467.9 3.0 multiply_convert_fusion.1
  470.9 1.2 multiply_convert_fusion.2
  472.0 55.6 %all-reduce.5.cloned.1.call-done = bf16[2,256,4,384]{1,3,2,0:T(8,128)(2,1)} async-done(((bf16[2,256,4,384]{1,3,2,0:T(8,128)(2,1)}), bf16[2,256,4,384]{1,3,2,0:T(8,128)(2,1)}) %all-reduce.5.cloned.1.call-update) | async-done | bytes 1572880 | tf_op jit(solution)/shard_map/psum | solution.py:119
  527.7 3.9 copy.100
  531.5 0.6 copy.91
  532.2 0.6 copy.92
  533.1 2.6 fusion.18
  535.7 76.1 %all-reduce = (f32[384]{0:T(512)}, f32[384]{0:T(512)}) all-reduce(f32[384]{0:T(512)} %get-tuple-element.28, f32[384]{0:T(512)S(1)} %copy-done.27), channel_id=1, replica_groups=mesh['copy'=4,'space'=64] {'copy','space'}, use_global_device_ids=true, to_apply=%region_12.13 | all-reduce | flops 768 | bytes 6144 | tf_op jit(solution)/shard_map/psum | solution.py:123
  611.8 1.3 broadcast_multiply_fusion.7
  613.1 1.3 broadcast_multiply_fusion.8
  614.4 0.7 broadcast_multiply_fusion.2
  615.1 3.4 fusion.17
  618.5 2.4 copy.98
  620.9 1.2 copy.99
  (82 shorter events, 6.1 us)
Async XLA Ops:
  7.2 125.9 %copy-start = (bf16[384,1536]{1,0:T(8,128)(2,1)S(1)}, bf16[384,1536]{1,0:T(8,128)(2,1)}, u32[]{:S(2)}) copy-start(bf16[384,1536]{1,0:T(8,128)(2,1)} %param.10) | copy-start | bytes 3538948
  10.5 1.8 copy-start.28
  11.9 0.9 copy-start.13
  11.9 1.0 copy-start.15
  12.8 3.7 copy-start.25
  16.5 52.1 %all-to-all-start = ((bf16[2,1,4,256,384]{4,0,2,1,3:T(2,128)(2,1)}), bf16[2,1,4,256,384]{4,0,2,1,3:T(2,128)(2,1)}, u32[]{:S(2)}, u32[]{:S(2)}) async-start(bf16[2,1,4,256,384]{4,0,2,1,3:T(2,128)(2,1)} %copy.69), calls=%async_computation | async-start | bytes 3145728 | tf_op jit(solution)/shard_map/all_to_all | solution.py:75
  33.8 40.6 %copy-start.4 = (bf16[1,256,4,384]{1,3,2,0:T(8,128)(2,1)}, bf16[1,256,4,384]{1,3,2,0:T(8,128)(2,1)S(1)}, u32[]{:S(2)}) copy-start(bf16[1,256,4,384]{1,3,2,0:T(8,128)(2,1)S(1)} %copy.124) | copy-start | bytes 2359300
  35.6 38.8 %copy-start.6 = (bf16[1,256,4,384]{1,3,2,0:T(8,128)(2,1)}, bf16[1,256,4,384]{1,3,2,0:T(8,128)(2,1)S(1)}, u32[]{:S(2)}) copy-start(bf16[1,256,4,384]{1,3,2,0:T(8,128)(2,1)S(1)} %copy.126) | copy-start | bytes 2359300
  70.6 1.0 copy-start.11
  70.6 1.0 copy-start.12
  74.4 1.0 copy-start.20
  74.4 1.0 copy-start.22
  132.0 0.7 copy-start.24
  133.0 15.5 %copy-start.19 = (bf16[1,4,256,384]{3,2,1,0:T(8,128)(2,1)}, bf16[1,4,256,384]{3,2,1,0:T(8,128)(2,1)S(1)}, u32[]{:S(2)}) copy-start(bf16[1,4,256,384]{3,2,1,0:T(8,128)(2,1)S(1)} %multiply_convert_fusion.4) | copy-start | bytes 2359300
  133.0 15.5 %copy-start.17 = (bf16[1,4,256,384]{3,2,1,0:T(8,128)(2,1)S(1)}, bf16[1,4,256,384]{3,2,1,0:T(8,128)(2,1)}, u32[]{:S(2)}) copy-start(bf16[1,4,256,384]{3,2,1,0:T(8,128)(2,1)} %param.8) | copy-start | bytes 2359300
  133.1 15.5 %copy-start.30 = (bf16[1536,384]{1,0:T(8,128)(2,1)S(1)}, bf16[1536,384]{1,0:T(8,128)(2,1)}, u32[]{:S(2)}) copy-start(bf16[1536,384]{1,0:T(8,128)(2,1)} %param.11) | copy-start | bytes 3538948
  151.8 1.9 copy-start.31
  153.8 1.2 copy-start.3
  166.2 47.4 %all-to-all-start.2 = ((bf16[2,1,4,256,384]{4,0,2,1,3:T(2,128)(2,1)}), bf16[2,1,4,256,384]{4,0,2,1,3:T(2,128)(2,1)S(1)}, u32[]{:S(2)}, u32[]{:S(2)}) async-start(bf16[2,1,4,256,384]{4,0,2,1,3:T(2,128)(2,1)} %copy.84), calls=%async_computation.2 | async-start | bytes 3145728 | tf_op jit(solution)/shard_map/all_to_all | solution.py:75
  173.9 293.9 %all-reduce.7.cloned.1.call-start = ((), (), s32[]{:S(2)}) async-start(), calls=%async_computation.5 | async-start | bytes 9437184 | tf_op jit(solution)/shard_map/psum | solution.py:123
  174.1 5.2 copy-start.18
  174.1 5.2 copy-start.32
  217.5 4.3 copy-start.5
  217.5 4.3 copy-start.7
  221.8 1.0 copy-start.21
  221.8 1.0 copy-start.23
  227.0 304.5 %all-to-all-start.3 = ((bf16[2,1,256,4,384]{4,0,3,1,2:T(2,128)(2,1)}), bf16[2,1,256,4,384]{4,0,3,1,2:T(2,128)(2,1)S(1)}, u32[]{:S(2)}, u32[]{:S(2)}) async-start(bf16[2,1,256,4,384]{4,0,3,1,2:T(2,128)(2,1)} %copy.90), calls=%async_computation.3 | async-start | bytes 3145728 | tf_op jit(solution)/shard_map/all_to_all | solution.py:84
  235.3 292.3 %all-reduce.5.cloned.1.call-start = ((), (), s32[]{:S(2)}) async-start(), calls=%async_computation.4 | async-start | bytes 3145728 | tf_op jit(solution)/shard_map/psum | solution.py:119
  235.6 3.9 copy-start.1
  235.6 4.8 copy-start.2
  467.8 3.0 copy-start.10
  532.1 0.9 copy-start.14
  532.2 1.0 copy-start.16
  532.2 1.0 copy-start.26
  532.2 0.9 copy-start.29
  533.1 2.6 copy-start.27
  533.1 81.9 %copy-start.8 = (f32[1,4,256,384]{2,3,1,0:T(8,128)S(1)}, f32[1,4,256,384]{2,3,1,0:T(8,128)}, u32[]{:S(2)}) copy-start(f32[1,4,256,384]{2,3,1,0:T(8,128)} %copy.81) | copy-start | bytes 4718596
  618.5 2.4 copy-start.9
Sparse Core Ops, SparseCore 0:
  182.7 285.0 all-reduce.6
  470.7 56.9 all-reduce.4
where the time goes:
time: 639 us; the launch traced here: 629 us
  waiting for transfers between devices  332 us (52%)
  blocking collectives  121 us (19%)
  matrix products  53.9 us (8%)
  local copies, waits for them, and re-layouts  50 us (8%)
  starting transfers between devices  30.3 us (5%)
  other arithmetic  27.3 us (4%)
  between operations  14.7 us (2%)
    psum x1, waiting for transfers between devices, body(): lax.psum((local_sums[0], local_sums[1], local_sums[2], local_sums[3]), ('...  215 us
    psum x1, blocking collectives, body(): lax.psum((local_sums[0], local_sums[1], local_sums[2], local_sums[3]), ('...  76.1 us
    all_to_all x2, waiting for transfers between devices, spectral(): lax.all_to_all(rows, 'space', split_axis=3, concat_axis=2, tiled=True)  61 us
    psum x1, waiting for transfers between devices, body(): lax.psum(filter_terms.astype(jnp.bfloat16), 'copy').astype(jnp.float32)  55.6 us
    all_to_all x1, blocking collectives, spectral(): lax.all_to_all(returned, 'space', split_axis=2, concat_axis=3, tiled=True)  45.2 us
    all_to_all x2, starting transfers between devices, spectral(): lax.all_to_all(rows, 'space', split_axis=3, concat_axis=2, tiled=True)  21.5 us
    unnamed x73, local copies, waits for them, and re-layouts  17.3 us
    dot_general x1, matrix products, body(): preact = jnp.dot(mlp_in, weight_in, preferred_element_type=jnp.float32)  15.5 us
  transfers between devices with their start and end apart: 5, of which 4 were waited for; matrix products, arithmetic and copies ran while one was open for 9% of the time, Pallas kernels for 0%

commit v1 on v0

--- a/solution.py
+++ b/solution.py
@@ -116,7 +116,9 @@
             jnp.sum(adj_f[1] * spec_f[0] - adj_f[0] * spec_f[1], axis=0),
         ]
     )
-    grad_filter = lax.psum(filter_terms.astype(jnp.bfloat16), "copy").astype(jnp.float32)
+    grad_filter = jnp.sum(lax.all_gather(filter_terms.astype(jnp.bfloat16), "copy"), axis=0).astype(
+        jnp.float32
+    )
     grad_normed, sum_gain_one = norm_backward(back_spatial, normed_one, rstd_one, gain_one)
     grad_tokens = (grad_out.astype(jnp.float32) + grad_normed).astype(jnp.bfloat16)
     local_sums = (sum_in, sum_out, sum_gain_one, sum_gain_two)

time: 639 us -> 616 us (0.964)
  waiting for transfers between devices: 332 us -> 317 us
    psum x1 -> x0, waiting for transfers between devices: 55.6 us -> none  [body(): lax.psum(filter_terms.astype(jnp.bfloat16), 'copy').astype(jnp.float32)]
    psum x1, waiting for transfers between devices: 215 us -> 256 us  [body(): lax.psum((local_sums[0], local_sums[1], local_sums[2], local_sums[3]), ('...]
    unnamed x73 -> x75, local copies, waits for them, and re-layouts: 17.3 us -> 15.4 us
  transfers between devices with their start and end apart: 5 -> 5, of which waited for: 4 -> 3; matrix products, arithmetic and copies ran while one was open for 9% -> 8% of each run, Pallas kernels for 0% -> 0%
where the time goes in v1:
time: 616 us; the launch traced here: 607 us
  waiting for transfers between devices  317 us (51%)
  blocking collectives  123 us (20%)
  matrix products  50.2 us (8%)
  local copies, waits for them, and re-layouts  45.4 us (7%)
  starting transfers between devices  30.2 us (5%)
  other arithmetic  24.4 us (4%)
  between operations  16.2 us (3%)
    psum x1, waiting for transfers between devices, body(): lax.psum((local_sums[0], local_sums[1], local_sums[2], local_sums[3]), ('...  256 us
    psum x1, blocking collectives, body(): lax.psum((local_sums[0], local_sums[1], local_sums[2], local_sums[3]), ('...  77.8 us
    all_to_all x2, waiting for transfers between devices, spectral(): lax.all_to_all(rows, 'space', split_axis=3, concat_axis=2, tiled=True)  61.1 us
    all_to_all x1, blocking collectives, spectral(): lax.all_to_all(returned, 'space', split_axis=2, concat_axis=3, tiled=True)  45.2 us
    all_to_all x2, starting transfers between devices, spectral(): lax.all_to_all(rows, 'space', split_axis=3, concat_axis=2, tiled=True)  21.5 us
    dot_general x1, matrix products, body(): preact = jnp.dot(mlp_in, weight_in, preferred_element_type=jnp.float32)  15.5 us
    unnamed x75, local copies, waits for them, and re-layouts  15.4 us
  transfers between devices with their start and end apart: 5, of which 3 were waited for; matrix products, arithmetic and copies ran while one was open for 8% of the time, Pallas kernels for 0%

profile of v1, /device:TPU:1, one launch (start us, length us, event | category | flops | bytes accessed | tf_op | source)
XLA Modules:
  0.0 606.8 jit_solution(4714788871624768242)
XLA Ops:
  8.0 1.6 fusion.79
  9.7 1.6 multiply_convert_fusion.8
  11.3 1.4 copy.57
  13.7 0.6 fusion.35
  14.3 3.0 copy.59
  17.3 13.8 %all-to-all-start = ((bf16[2,1,4,256,384]{4,0,2,1,3:T(2,128)(2,1)}), bf16[2,1,4,256,384]{4,0,2,1,3:T(2,128)(2,1)}, u32[]{:S(2)}, u32[]{:S(2)}) async-start(bf16[2,1,4,256,384]{4,0,2,1,3:T(2,128)(2,1)} %copy.59), calls=%async_computation | async-start | bytes 3145728 | tf_op jit(solution)/shard_map/all_to_all | solution.py:75
  31.2 2.8 fusion.86
  34.0 0.6 copy.111
  34.6 1.8 copy.113
  36.5 1.0 broadcast_multiply_fusion
  37.5 1.1 multiply_convert_fusion.5
  38.6 1.0 fusion.66
  39.6 29.9 %all-to-all-done = bf16[2,1,4,256,384]{4,0,2,1,3:T(2,128)(2,1)} async-done(((bf16[2,1,4,256,384]{4,0,2,1,3:T(2,128)(2,1)}), bf16[2,1,4,256,384]{4,0,2,1,3:T(2,128)(2,1)}, u32[]{:S(2)}, u32[]{:S(2)}) %all-to-all-start) | async-done | bytes 1572896 | tf_op jit(solution)/shard_map/all_to_all | solution.py:75
  69.5 2.0 copy.60
  71.5 0.6 copy.61
  72.5 2.7 fusion.87
  75.2 0.6 fusion.26
  76.2 2.2 fusion.40
  78.4 4.3 copy.67
  82.8 45.2 %all_to_all.60 = bf16[2,1,256,4,384]{4,0,3,1,2:T(2,128)(2,1)S(1)} all-to-all(bf16[2,1,256,4,384]{4,0,3,1,2:T(2,128)(2,1)S(1)} %copy.67), channel_id=1, replica_groups=mesh['copy'=4,'space'=64] {'space'}, dimensions={2} | all-to-all | bytes 3145728 | tf_op jit(solution)/shard_map/all_to_all | solution.py:84
  128.0 0.6 copy.68
  128.6 0.5 copy.69
  129.2 1.4 reshape.532
  130.5 2.3 bitcast_reduce_fusion
  133.9 15.5 %multiply_convert_fusion = (bf16[1024,1536]{1,0:T(8,128)(2,1)}, f32[1024,1536]{1,0:T(8,128)S(1)}, f32[1024,1536]{1,0:T(8,128)S(1)}) fusion(bf16[1024,384]{1,0:T(8,128)(2,1)S(1)} %bitcast.216, bf16[384,1536]{1,0:T(8,128)(2,1)S(1)} %copy-done), kind=kOutput, calls=%fused_computation.3 | convolution fusion | flops 1310195712 | bytes 17694720 | tf_op jit(solution)/shard_map/dot_general | solution.py:97
  149.4 3.3 add_convert_fusion
  152.7 1.9 multiply_reduce_fusion.2
  154.6 1.1 multiply_reduce_fusion
  155.8 0.6 broadcast_multiply_fusion.4
  156.4 0.6 broadcast_multiply_fusion.1
  157.0 1.3 div.31
  158.2 3.9 fusion.36
  162.1 5.0 copy.74
  167.1 7.6 %all-to-all-start.2 = ((bf16[2,1,4,256,384]{4,0,2,1,3:T(2,128)(2,1)}), bf16[2,1,4,256,384]{4,0,2,1,3:T(2,128)(2,1)S(1)}, u32[]{:S(2)}, u32[]{:S(2)}) async-start(bf16[2,1,4,256,384]{4,0,2,1,3:T(2,128)(2,1)} %copy.74), calls=%async_computation.2 | async-start | bytes 3145728 | tf_op jit(solution)/shard_map/all_to_all | solution.py:75
  175.0 5.1 fusion.90
  180.1 3.3 fusion.91
  183.4 31.2 %all-to-all-done.2 = bf16[2,1,4,256,384]{4,0,2,1,3:T(2,128)(2,1)S(1)} async-done(((bf16[2,1,4,256,384]{4,0,2,1,3:T(2,128)(2,1)}), bf16[2,1,4,256,384]{4,0,2,1,3:T(2,128)(2,1)S(1)}, u32[]{:S(2)}, u32[]{:S(2)}) %all-to-all-start.2) | async-done | bytes 1572896 | tf_op jit(solution)/shard_map/all_to_all | solution.py:75
  214.6 0.6 copy.75
  215.3 0.6 copy.76
  216.3 2.2 fusion.88
  218.5 0.5 add_convert_fusion.1
  219.0 1.3 pad_maximum_fusion
  220.3 1.1 copy-done.4
  221.7 2.1 fusion.21
  223.8 1.0 fusion.46
  224.8 3.0 copy.80
  227.9 8.5 %all-to-all-start.3 = ((bf16[2,1,256,4,384]{4,0,3,1,2:T(2,128)(2,1)}), bf16[2,1,256,4,384]{4,0,3,1,2:T(2,128)(2,1)S(1)}, u32[]{:S(2)}, u32[]{:S(2)}) async-start(bf16[2,1,256,4,384]{4,0,3,1,2:T(2,128)(2,1)} %copy.80), calls=%async_computation.3 | async-start | bytes 3145728 | tf_op jit(solution)/shard_map/all_to_all | solution.py:84
  236.3 2.4 copy.72
  238.7 5.2 fusion.89
  244.0 3.0 copy.71
  247.0 256.4 %all-reduce.4.cloned.1.call-done = (f32[384,1536]{1,0:T(8,128)}, f32[1536,384]{1,0:T(8,128)}) async-done(((f32[384,1536]{1,0:T(8,128)}, f32[1536,384]{1,0:T(8,128)}), (f32[384,1536]{1,0:T(8,128)}, f32[1536,384]{1,0:T(8,128)})) %all-reduce.4.cloned.1.call-update) | async-done | bytes 4718608 | tf_op jit(solution)/shard_map/psum | solution.py:125
  503.3 3.0 multiply_convert_fusion.1
  506.4 1.2 multiply_convert_fusion.2
  507.5 0.6 copy.81
  508.2 0.6 copy.82
  509.1 1.0 fusion.18
  510.7 0.8 fusion.17
  511.5 1.2 copy.84
  512.7 1.2 copy.85
  513.8 77.8 %all-reduce = (f32[384]{0:T(512)S(1)}, f32[384]{0:T(512)S(1)}) all-reduce(f32[384]{0:T(512)S(1)} %get-tuple-element.28, f32[384]{0:T(512)S(1)} %copy-done.28), channel_id=1, replica_groups=mesh['copy'=4,'space'=64] {'copy','space'}, use_global_device_ids=true, to_apply=%region_12.13 | all-reduce | flops 768 | bytes 6144 | tf_op jit(solution)/shard_map/psum | solution.py:125
  591.6 0.6 broadcast_multiply_fusion.7
  592.2 0.6 broadcast_multiply_fusion.8
  592.8 3.9 reduce_sum.118
  596.7 2.4 copy.86
  (83 shorter events, 4.7 us)
Async XLA Ops:
  8.0 125.9 %copy-start = (bf16[384,1536]{1,0:T(8,128)(2,1)S(1)}, bf16[384,1536]{1,0:T(8,128)(2,1)}, u32[]{:S(2)}) copy-start(bf16[384,1536]{1,0:T(8,128)(2,1)} %param.10) | copy-start | bytes 3538948
  11.3 1.8 copy-start.29
  12.7 0.9 copy-start.14
  12.7 1.0 copy-start.16
  13.7 3.7 copy-start.26
  17.3 52.1 %all-to-all-start = ((bf16[2,1,4,256,384]{4,0,2,1,3:T(2,128)(2,1)}), bf16[2,1,4,256,384]{4,0,2,1,3:T(2,128)(2,1)}, u32[]{:S(2)}, u32[]{:S(2)}) async-start(bf16[2,1,4,256,384]{4,0,2,1,3:T(2,128)(2,1)} %copy.59), calls=%async_computation | async-start | bytes 3145728 | tf_op jit(solution)/shard_map/all_to_all | solution.py:75
  34.6 40.6 %copy-start.3 = (bf16[1,256,4,384]{1,3,2,0:T(8,128)(2,1)}, bf16[1,256,4,384]{1,3,2,0:T(8,128)(2,1)S(1)}, u32[]{:S(2)}) copy-start(bf16[1,256,4,384]{1,3,2,0:T(8,128)(2,1)S(1)} %copy.111) | copy-start | bytes 2359300
  36.5 38.8 %copy-start.5 = (bf16[1,256,4,384]{1,3,2,0:T(8,128)(2,1)}, bf16[1,256,4,384]{1,3,2,0:T(8,128)(2,1)S(1)}, u32[]{:S(2)}) copy-start(bf16[1,256,4,384]{1,3,2,0:T(8,128)(2,1)S(1)} %copy.113) | copy-start | bytes 2359300
  71.5 1.0 copy-start.10
  71.5 1.0 copy-start.12
  75.2 1.0 copy-start.21
  75.2 1.0 copy-start.23
  132.8 0.7 copy-start.25
  133.8 15.6 %copy-start.20 = (bf16[1,4,256,384]{3,2,1,0:T(8,128)(2,1)}, bf16[1,4,256,384]{3,2,1,0:T(8,128)(2,1)S(1)}, u32[]{:S(2)}) copy-start(bf16[1,4,256,384]{3,2,1,0:T(8,128)(2,1)S(1)} %multiply_convert_fusion.4) | copy-start | bytes 2359300
  133.9 15.5 %copy-start.18 = (bf16[1,4,256,384]{3,2,1,0:T(8,128)(2,1)S(1)}, bf16[1,4,256,384]{3,2,1,0:T(8,128)(2,1)}, u32[]{:S(2)}) copy-start(bf16[1,4,256,384]{3,2,1,0:T(8,128)(2,1)} %param.8) | copy-start | bytes 2359300
  133.9 15.5 %copy-start.31 = (bf16[1536,384]{1,0:T(8,128)(2,1)S(1)}, bf16[1536,384]{1,0:T(8,128)(2,1)}, u32[]{:S(2)}) copy-start(bf16[1536,384]{1,0:T(8,128)(2,1)} %param.11) | copy-start | bytes 3538948
  152.7 1.9 copy-start.32
  154.6 1.2 copy-start.1
  167.1 47.5 %all-to-all-start.2 = ((bf16[2,1,4,256,384]{4,0,2,1,3:T(2,128)(2,1)}), bf16[2,1,4,256,384]{4,0,2,1,3:T(2,128)(2,1)S(1)}, u32[]{:S(2)}, u32[]{:S(2)}) async-start(bf16[2,1,4,256,384]{4,0,2,1,3:T(2,128)(2,1)} %copy.74), calls=%async_computation.2 | async-start | bytes 3145728 | tf_op jit(solution)/shard_map/all_to_all | solution.py:75
  174.7 328.6 %all-reduce.4.cloned.1.call-start = ((), (), s32[]{:S(2)}) async-start(), calls=%async_computation.5 | async-start | bytes 9437184 | tf_op jit(solution)/shard_map/psum | solution.py:125
  175.0 5.1 copy-start.19
  175.0 5.1 copy-start.33
  183.4 409.4 %all-gather.2.cloned.1.call-start = ((), (), s32[]{:S(2)}) async-start(), calls=%async_computation.4 | async-start | bytes 7864320 | tf_op jit(solution)/shard_map/all_gather | solution.py:119
  215.2 1.0 copy-start.11
  215.2 1.0 copy-start.13
  216.3 2.2 copy-start.2
  220.3 1.1 copy-start.4
  220.3 1.4 copy-start.6
  221.7 2.1 copy-start.22
  221.7 2.1 copy-start.24
  227.9 279.7 %all-to-all-start.3 = ((bf16[2,1,256,4,384]{4,0,3,1,2:T(2,128)(2,1)}), bf16[2,1,256,4,384]{4,0,3,1,2:T(2,128)(2,1)S(1)}, u32[]{:S(2)}, u32[]{:S(2)}) async-start(bf16[2,1,256,4,384]{4,0,3,1,2:T(2,128)(2,1)} %copy.80), calls=%async_computation.3 | async-start | bytes 3145728 | tf_op jit(solution)/shard_map/all_to_all | solution.py:84
  503.3 3.0 copy-start.9
  508.1 0.9 copy-start.15
  508.1 1.0 copy-start.17
  508.1 1.0 copy-start.27
  508.2 0.9 copy-start.30
  509.1 1.4 copy-start.7
  509.1 1.6 copy-start.8
  511.5 2.3 copy-start.28
Sparse Core Ops, SparseCore 0:
  183.5 319.7 all-reduce.3
Sparse Core Ops, SparseCore 1:
  220.4 70.0 all-gather.1
